TPU v7x, 128 devices: a whole 4x4x4 slice. The times are simulated.
128 devices in a mesh: section: 2 (over core), dp: 16 (over y, x), mp: 4 (over z).
Axes of the slice: x: 4, y: 4, z: 4, core: 2. Of those that a mesh axis runs over, the one named last changes fastest.
Arguments:
- patches: bfloat16 [8192, 1280], P(('section', 'dp', 'mp')), may hold values from -6 to 6
- image_units: int32 [128, 3], P(('section', 'dp', 'mp')), may hold values from 1 to 8, 16 in all within a row
- v_gain: float32 [1280], replicated, may hold values from 0.5 to 1.5
- v_qkv: bfloat16 [1280, 3840], replicated, may hold values from -0.15625 to 0.15625
- v_out: bfloat16 [1280, 1280], replicated, may hold values from -0.15625 to 0.15625
- merge_gain: float32 [1280], replicated, may hold values from 0.5 to 1.5
- w_merge: bfloat16 [5120, 8192], P('dp', 'mp'), may hold values from -0.078125 to 0.078125
- routes: int32 [2048, 1], P(('section', 'dp', 'mp')), may hold values from 0 to 15; in each aligned block of 1024 rows (0 to 1023, 1024 to 2047, ...) at most 128 rows name the same one
- text: bfloat16 [4096, 8192], P(('section', 'dp'), 'mp'), may hold values from -6 to 6
- seq_lengths: int32 [32, 3], P(('section', 'dp')), may hold values from 1 to 64, 128 in all within a row
- lang_gain: float32 [2, 8192], P('section'), may hold values from 0.5 to 1.5
- w_qkv: bfloat16 [2, 8192, 5120], P('section', 'dp', 'mp'), may hold values from -0.0625 to 0.0625
- wo_t: bfloat16 [2, 8192, 4096], P('section', 'dp', 'mp'), may hold values from -0.09375 to 0.09375
- row_grads: bfloat16 [4096, 8192], P(('section', 'dp'), 'mp'), may hold values from -6 to 6
Outputs:
- final_hidden: bfloat16 [4096, 8192], P(('section', 'dp'), 'mp')
- merged_grads: bfloat16 [2048, 8192], P(('section', 'dp', 'mp'))
Inputs may be any that keep to these rules, and one draw needn't show every extreme that they name: `image_units`: each row sums to 16. `routes`: among the 1024 rows of one section index (aligned blocks), at most 128 name one group; in some section index one group is named by exactly 128. `seq_lengths`: each row sums to 128.
All inputs are finite; a program needn't handle non-finite values.
Results may differ from a plain program's by a relative error of at most 0.03.
Values may be sent and summed in bfloat16 or wider, within the bound.
A program may use at most 192 MiB of HBM per device.

v0:
```python
import math
import jax
import jax.numpy as jnp
from jax import lax
from jax.sharding import PartitionSpec as P

QH = 32
KVH = 4
HD = 128
VD = 1280
VH = 16
VHD = 80
MERGE = 4
EPSILON = 1e-06


def passed_along(value, axis, steps):
    count = lax.axis_size(axis)
    initial, last = (max(0, -steps), min(count, count - steps))
    return lax.ppermute(value, axis, [(source, source + steps) for source in range(initial, last)])


def broadcast(block, axis, owner):
    block = jnp.where(lax.axis_index(axis) == owner, block, jnp.zeros_like(block))
    return lax.psum(block, axis)


def layer_norm(values, norm_gain):
    values = values.astype(jnp.float32)
    centre = jnp.mean(values, axis=-1, keepdims=True)
    centred = values - centre
    variance = jnp.mean(centred * centred, axis=-1, keepdims=True)
    return centred * lax.rsqrt(variance + EPSILON) * norm_gain


def rms_norm(values, norm_gain):
    values = values.astype(jnp.float32)
    return (
        values * lax.rsqrt(jnp.mean(values * values, axis=-1, keepdims=True) + EPSILON) * norm_gain
    )


def segment_of(lengths, amount):
    boundary = jnp.cumsum(lengths.astype(jnp.int32))
    positions = jnp.arange(amount, dtype=jnp.int32)
    return jnp.sum((positions[:, None] >= boundary[None, :]).astype(jnp.int32), axis=1)


def vision_rows(patches, units, v_gain, v_qkv, v_out, merge_gain):
    amount = patches.shape[0]
    merged_count = amount // MERGE
    unit_image = segment_of(units, merged_count)
    image_ids = jnp.broadcast_to(unit_image[:, None], (merged_count, MERGE)).reshape(amount)
    v_normed = layer_norm(patches, v_gain).astype(jnp.bfloat16)
    projected = jnp.dot(v_normed, v_qkv, preferred_element_type=jnp.float32).astype(jnp.bfloat16)
    projected = projected.reshape(amount, 3, VH, VHD)
    scores = jnp.einsum(
        "qhd,khd->hqk", projected[:, 0], projected[:, 1], preferred_element_type=jnp.float32
    ) / math.sqrt(VHD)
    allowed = image_ids[:, None] == image_ids[None, :]
    scores = jnp.where(allowed[None], scores, -1e30)
    weights = jax.nn.softmax(scores, axis=-1).astype(jnp.bfloat16)
    attended = (
        jnp.einsum("hqk,khd->qhd", weights, projected[:, 2], preferred_element_type=jnp.float32)
        .astype(jnp.bfloat16)
        .reshape(amount, VD)
    )
    update = jnp.dot(attended, v_out, preferred_element_type=jnp.float32)
    v_hidden = (patches.astype(jnp.float32) + update).astype(jnp.bfloat16)
    merged = layer_norm(v_hidden, merge_gain).astype(jnp.bfloat16)
    return merged.reshape(merged_count, MERGE * VD)


def attend(projected, lengths):
    seq_rows = projected.shape[0]
    group_size = QH // KVH
    kv_here = projected.shape[1] // ((group_size + 2) * HD)
    heads_view = projected.reshape(seq_rows, kv_here, group_size + 2, HD)
    scores = jnp.einsum(
        "tkgd,skd->kgts",
        heads_view[:, :, :group_size],
        heads_view[:, :, group_size],
        preferred_element_type=jnp.float32,
    ) * (1.0 / math.sqrt(HD))
    seq_ids = segment_of(lengths, seq_rows)
    positions = jnp.arange(seq_rows, dtype=jnp.int32)
    allowed = (seq_ids[:, None] == seq_ids[None, :]) & (positions[:, None] >= positions[None, :])
    scores = jnp.where(allowed[None, None], scores, -1e30)
    weights = jax.nn.softmax(scores, axis=-1).astype(jnp.bfloat16)
    attended = jnp.einsum(
        "kgts,skd->tkgd",
        weights,
        heads_view[:, :, group_size + 1],
        preferred_element_type=jnp.float32,
    ).astype(jnp.bfloat16)
    return attended.reshape(seq_rows, kv_here * group_size * HD)


def shards(
    patches,
    image_units,
    v_gain,
    v_qkv,
    v_out,
    merge_gain,
    w_merge,
    routes,
    text,
    seq_lengths,
    lang_gain,
    w_qkv,
    wo_t,
    row_grads,
):
    merged = vision_rows(patches, image_units[0], v_gain, v_qkv, v_out, merge_gain)
    all_rows, all_routes = (
        lax.all_gather(merged, ("dp", "mp"), axis=0, tiled=True),
        lax.all_gather(routes, ("dp", "mp"), axis=0, tiled=True),
    )
    target = all_routes[:, 0]
    section_rows = target.shape[0]
    row_order = jnp.arange(section_rows, dtype=jnp.int32)
    matching = target[:, None] == target[None, :]
    position = jnp.sum(
        (matching & (row_order[:, None] > row_order[None, :])).astype(jnp.int32), axis=1
    )
    seq_rows = text.shape[0]
    slot_index = target * seq_rows + position
    group_here = lax.axis_index("dp")
    dp_count = lax.axis_size("dp")
    slice_width = w_merge.shape[0]
    row_slice = lax.dynamic_slice_in_dim(all_rows, group_here * slice_width, slice_width, 1)
    wanted = jnp.arange(seq_rows * lax.axis_size("dp"), dtype=jnp.int32)
    picker = (slot_index[None, :] == wanted[:, None]).astype(jnp.bfloat16)
    picked = jnp.dot(picker, row_slice, preferred_element_type=jnp.float32).astype(jnp.bfloat16)
    image_rows = lax.psum_scatter(
        jnp.dot(picked, w_merge, preferred_element_type=jnp.float32).astype(jnp.bfloat16),
        "dp",
        scatter_dimension=0,
        tiled=True,
    )
    present = jnp.sum((target == group_here).astype(jnp.int32))
    positions = jnp.arange(seq_rows, dtype=jnp.int32)
    entry_rows = jnp.where((positions < present)[:, None], image_rows, text)
    gathered = (
        lax.all_gather(w_qkv, "dp", axis=1, tiled=True),
        lax.all_gather(wo_t, "dp", axis=1, tiled=True),
    )
    qkv_weight = gathered[0][0]
    out_weight = gathered[1][0]
    norm_gain = lang_gain[0]
    sections = lax.axis_size("section")
    section_here = lax.axis_index("section")
    is_first = section_here == 0
    lengths_here = seq_lengths[0]
    entry_all, lengths_all = (
        lax.all_gather(entry_rows, "section", axis=0, tiled=True),
        lax.all_gather(seq_lengths, "section", axis=0, tiled=True),
    )
    carried = jnp.zeros_like(entry_rows)
    carried_lengths = lengths_here
    finished = []
    for section_step in range(2 * sections - 1):
        if section_step > 0:
            carried, carried_lengths = passed_along((carried, carried_lengths), "section", 1)
        if section_step < sections:
            incoming = entry_all[section_step * seq_rows : (section_step + 1) * seq_rows]
            incoming_lengths = lengths_all[section_step]
            carried = jnp.where(is_first, incoming, carried)
            carried_lengths = jnp.where(is_first, incoming_lengths, carried_lengths)
        features = lax.all_gather(carried, "mp", axis=1, tiled=True)
        normed = rms_norm(features, norm_gain).astype(jnp.bfloat16)
        projected = jnp.dot(normed, qkv_weight, preferred_element_type=jnp.float32)
        attended = attend(projected.astype(jnp.bfloat16), carried_lengths)
        partial_value = lax.dot_general(
            attended, out_weight, (((1,), (1,)), ((), ())), preferred_element_type=jnp.float32
        )
        update = lax.psum_scatter(
            partial_value.astype(jnp.bfloat16), "mp", scatter_dimension=1, tiled=True
        ).astype(jnp.float32)
        carried = (carried.astype(jnp.float32) + update).astype(jnp.bfloat16)
        if section_step >= sections - 1:
            finished.append(carried)
    returned_rows = broadcast(jnp.stack(finished), "section", sections - 1)
    final_hidden = lax.dynamic_index_in_dim(returned_rows, section_here, 0, keepdims=False)
    columns = row_grads.shape[1]
    picker = ((target == group_here)[:, None] & (position[:, None] == positions[None, :])).astype(
        jnp.bfloat16
    )
    outgoing = jnp.dot(picker, row_grads, preferred_element_type=jnp.float32).astype(jnp.bfloat16)
    outgoing = outgoing.reshape(dp_count, section_rows // dp_count, columns)
    returned = lax.all_to_all(
        lax.all_to_all(outgoing, "dp", split_axis=0, concat_axis=0, tiled=True),
        "mp",
        split_axis=1,
        concat_axis=2,
        tiled=True,
    )
    merged_grads = jnp.sum(returned.astype(jnp.float32), axis=0).astype(jnp.bfloat16)
    return (final_hidden, merged_grads)


def solution(mesh):
    in_specs = (
        P(("section", "dp", "mp"), None),
        P(("section", "dp", "mp"), None),
        P(),
        P(),
        P(),
        P(),
        P("dp", "mp"),
        P(("section", "dp", "mp"), None),
        P(("section", "dp"), "mp"),
        P(("section", "dp"), None),
        P("section", None),
        P("section", "dp", "mp"),
        P("section", "dp", "mp"),
        P(("section", "dp"), "mp"),
    )
    out_specs = (P(("section", "dp"), "mp"), P(("section", "dp", "mp"), None))
    return jax.shard_map(shards, mesh=mesh, in_specs=in_specs, out_specs=out_specs, check_vma=False)
```

profile of v0, /device:TPU:0, one launch (start us, length us, event | category | flops | bytes accessed | tf_op | source)
XLA Modules:
  0.0 799.6 jit_solution(8067572202809848577)
XLA Ops:
  7.2 1.2 convert_reduce_fusion.1
  8.4 1.1 fusion.76
  9.6 6.6 convolution_convert_fusion.1
  16.2 3.1 reshape.446
  19.3 2.0 fusion.97
  21.8 1.3 fusion.60
  23.3 0.6 copy-done.15
  23.9 2.4 fusion.64
  26.3 1.8 copy.109
  28.1 1.9 reshape.449
  30.0 1.7 fusion.99
  32.1 0.8 reshape.450
  33.0 0.6 dynamic-slice
  34.4 24.9 %all-reduce = s32[1024]{0:T(1024)S(1)} all-reduce(s32[1024]{0:T(1024)S(1)} %bitcast_dynamic-update-slice_fusion), channel_id=1, replica_groups=mesh['section'=2,'dp'=16,'mp'=4] {'dp','mp'}, use_global_device_ids=true, to_apply=%add | all-reduce | flops 1024 | bytes 8192 | tf_op jit(solution)/shard_map/squeeze | solution.py:120
  59.8 0.6 convert_reduce_fusion.2
  60.4 60.5 %all-gather.9.cloned.1.call-done = bf16[1024,5120]{1,0:T(8,128)(2,1)} async-done(((bf16[16,5120]{1,0:T(8,128)(2,1)}), bf16[1024,5120]{1,0:T(8,128)(2,1)}) %all-gather.9.cloned.1.call-update) | async-done | bytes 10485776 | tf_op jit(solution)/shard_map/all_gather | solution.py:117
  120.9 10.7 %convolution_convert_fusion = bf16[2048,2048]{1,0:T(8,128)(2,1)} fusion(bf16[320,2048]{1,0:T(8,128)(2,1)} %param.20, s32[1024]{0:T(1024)S(1)} %get-tuple-element.7, bf16[1024,5120]{1,0:T(8,128)(2,1)} %all-gather.9.cloned.1.call-done, s32[]{:T(128)S(6)} %select_n.69), kind=kOutput, calls=%fused_computation.18 | convolution fusion | flops 4033478656 | bytes 10489860 | tf_op jit(solution)/shard_map/dot_general | solution.py:137
  131.7 0.7 iota_compare_fusion.13
  132.4 83.8 %reduce-scatter.5.cloned.1.call-done = bf16[128,2048]{1,0:T(8,128)(2,1)} async-done(((bf16[2048,2048]{1,0:T(8,128)(2,1)}), bf16[128,2048]{1,0:T(8,128)(2,1)}) %reduce-scatter.5.cloned.1.call-update) | async-done | bytes 524304 | tf_op jit(solution)/shard_map/reduce_scatter | solution.py:136
  216.3 2.0 broadcast_select_fusion
  218.3 11.4 %all-gather.11.cloned.1.call-done = bf16[256,2048]{1,0:T(8,128)(2,1)} async-done(((bf16[128,2048]{1,0:T(8,128)(2,1)}), bf16[256,2048]{1,0:T(8,128)(2,1)}) %all-gather.11.cloned.1.call-update) | async-done | bytes 1048592 | tf_op jit(solution)/shard_map/all_gather | solution.py:157
  229.7 1.9 slice_select_fusion
  231.6 0.5 all-gather.15.cloned.1.call-update
  232.8 2.2 all-gather
  235.4 28.8 %all-gather.13.cloned.1.call-done = bf16[128,8192]{1,0:T(8,128)(2,1)} async-done(((bf16[128,2048]{1,0:T(8,128)(2,1)}), bf16[128,8192]{1,0:T(8,128)(2,1)}) %all-gather.13.cloned.1.call-update) | async-done | bytes 2097168 | tf_op jit(solution)/shard_map/all_gather | solution.py:171
  264.2 2.1 fusion.23
  266.3 132.4 %all-gather.15.cloned.1.call-done = bf16[1,8192,1280]{2,1,0:T(8,128)(2,1)} async-done(((bf16[1,512,1280]{2,1,0:T(8,128)(2,1)}), bf16[1,8192,1280]{2,1,0:T(8,128)(2,1)}) %all-gather.15.cloned.1.call-update) | async-done | bytes 20971536 | tf_op jit(solution)/shard_map/all_gather | solution.py:146
  398.7 10.6 %fusion.35 = bf16[128,1280]{1,0:T(8,128)(2,1)S(1)} fusion(bf16[1,8192,1280]{2,1,0:T(8,128)(2,1)} %all-gather.15.cloned.1.call-done, bf16[128,8192]{1,0:T(8,128)(2,1)} %all-gather.13.cloned.1.call-done, f32[8192]{0:T(1024)S(1)} %bitcast.203, f32[128]{0:T(128)S(1)} %add_rsqrt_fusion.2), kind=kOutput, calls=%fused_computation.41 | convolution fusion | flops 2688712704 | bytes 23429632 | tf_op jit(solution)/shard_map/dot_general | solution.py:173
  410.1 101.6 %all-gather.17.cloned.1.call-done = bf16[1,8192,1024]{2,1,0:T(8,128)(2,1)} async-done(((bf16[1,512,1024]{2,1,0:T(8,128)(2,1)}), bf16[1,8192,1024]{2,1,0:T(8,128)(2,1)}) %all-gather.17.cloned.1.call-update) | async-done | bytes 16777232 | tf_op jit(solution)/shard_map/all_gather | solution.py:147
  511.7 12.8 %fusion.13 = bf16[128,8192]{1,0:T(8,128)(2,1)} fusion(bf16[128,1024]{0,1:T(8,128)(2,1)S(1)} %bitcast.197, bf16[1,8192,1024]{2,1,0:T(8,128)(2,1)} %all-gather.17.cloned.1.call-done), kind=kOutput, calls=%fused_computation.13 | convolution fusion | flops 2148532224 | bytes 19136512 | tf_op jit(solution)/shard_map/dot_general | solution.py:175
  524.6 29.7 %reduce-scatter.7.cloned.1.call-done = bf16[128,2048]{1,0:T(8,128)(2,1)} async-done(((bf16[128,8192]{1,0:T(8,128)(2,1)}), bf16[128,2048]{1,0:T(8,128)(2,1)}) %reduce-scatter.7.cloned.1.call-update) | async-done | bytes 524304 | tf_op jit(solution)/shard_map/reduce_scatter | solution.py:178
  554.3 1.2 add_convert_fusion.2
  555.5 1.8 collective-permute-start
  557.3 1.5 collective-permute-done
  558.8 0.8 slice_select_fusion.1
  559.8 2.5 collective-permute-start.1
  562.2 0.6 collective-permute-done.1
  563.2 27.3 %all-gather.19.cloned.1.call-done = bf16[128,8192]{1,0:T(8,128)(2,1)} async-done(((bf16[128,2048]{1,0:T(8,128)(2,1)}), bf16[128,8192]{1,0:T(8,128)(2,1)}) %all-gather.19.cloned.1.call-update) | async-done | bytes 2097168 | tf_op jit(solution)/shard_map/all_gather | solution.py:171
  590.5 2.1 fusion.26
  592.6 10.6 %fusion.38 = bf16[128,1280]{1,0:T(8,128)(2,1)S(1)} fusion(bf16[1,8192,1280]{2,1,0:T(8,128)(2,1)} %all-gather.15.cloned.1.call-done, bf16[128,8192]{1,0:T(8,128)(2,1)} %all-gather.19.cloned.1.call-done, f32[128]{0:T(128)S(1)} %add_rsqrt_fusion.1, f32[8192]{0:T(1024)S(1)} %bitcast.204), kind=kOutput, calls=%fused_computation.42 | convolution fusion | flops 2688712704 | bytes 23429632 | tf_op jit(solution)/shard_map/dot_general | solution.py:173
  604.0 12.8 %fusion.16 = bf16[128,8192]{1,0:T(8,128)(2,1)} fusion(bf16[128,1024]{0,1:T(8,128)(2,1)S(1)} %bitcast.199, bf16[1,8192,1024]{2,1,0:T(8,128)(2,1)} %all-gather.17.cloned.1.call-done), kind=kOutput, calls=%fused_computation.14 | convolution fusion | flops 2148532224 | bytes 19136512 | tf_op jit(solution)/shard_map/dot_general | solution.py:175
  616.9 29.9 %reduce-scatter.9.cloned.1.call-done = bf16[128,2048]{1,0:T(8,128)(2,1)} async-done(((bf16[128,8192]{1,0:T(8,128)(2,1)}), bf16[128,2048]{1,0:T(8,128)(2,1)}) %reduce-scatter.9.cloned.1.call-update) | async-done | bytes 524304 | tf_op jit(solution)/shard_map/reduce_scatter | solution.py:178
  646.8 1.2 add_convert_fusion.1
  648.0 1.8 collective-permute-start.2
  649.8 1.5 collective-permute-done.2
  651.3 0.8 copy-done.6
  652.1 3.1 convolution_convert_fusion.2
  655.2 6.9 all-to-all-start
  662.1 2.2 collective-permute-start.3
  664.3 0.6 collective-permute-done.3
  665.3 17.6 %all-gather.21.cloned.1.call-done = bf16[128,8192]{1,0:T(8,128)(2,1)} async-done(((bf16[128,2048]{1,0:T(8,128)(2,1)}), bf16[128,8192]{1,0:T(8,128)(2,1)}) %all-gather.21.cloned.1.call-update) | async-done | bytes 2097168 | tf_op jit(solution)/shard_map/all_gather | solution.py:171
  682.9 2.1 fusion.29
  685.0 10.6 %fusion.41 = bf16[128,1280]{1,0:T(8,128)(2,1)S(1)} fusion(bf16[1,8192,1280]{2,1,0:T(8,128)(2,1)} %all-gather.15.cloned.1.call-done, bf16[128,8192]{1,0:T(8,128)(2,1)} %all-gather.21.cloned.1.call-done, f32[128]{0:T(128)S(1)} %add_rsqrt_fusion, f32[8192]{0:T(1024)S(1)} %bitcast.205), kind=kOutput, calls=%fused_computation.43 | convolution fusion | flops 2688712704 | bytes 23429632 | tf_op jit(solution)/shard_map/dot_general | solution.py:173
  696.5 12.8 %fusion.19 = bf16[128,8192]{1,0:T(8,128)(2,1)} fusion(bf16[128,1024]{0,1:T(8,128)(2,1)S(1)} %bitcast.198, bf16[1,8192,1024]{2,1,0:T(8,128)(2,1)} %all-gather.17.cloned.1.call-done), kind=kOutput, calls=%fused_computation.15 | convolution fusion | flops 2148532224 | bytes 19136512 | tf_op jit(solution)/shard_map/dot_general | solution.py:175
  709.3 16.7 %all-to-all-done = bf16[16,64,2048]{2,1,0:T(8,128)(2,1)} async-done(((bf16[16,64,2048]{2,1,0:T(8,128)(2,1)}), bf16[16,64,2048]{2,1,0:T(8,128)(2,1)}, u32[]{:S(2)}, u32[]{:S(2)}) %all-to-all-start) | async-done | bytes 4194336 | tf_op jit(solution)/shard_map/all_to_all | solution.py:193
  726.0 6.5 copy.122
  732.5 5.0 all-to-all-start.1
  737.5 1.7 reduce-scatter.11.cloned.1.call-done
  739.2 1.2 fusion.68
  740.4 2.4 maximum_select_fusion
  742.8 43.2 %all-to-all-done.1 = bf16[16,64,2048]{2,0,1:T(8,128)(2,1)} async-done(((bf16[16,64,2048]{2,0,1:T(8,128)(2,1)}), bf16[16,64,2048]{2,0,1:T(8,128)(2,1)}, u32[]{:S(2)}, u32[]{:S(2)}) %all-to-all-start.1) | async-done | bytes 4194336 | tf_op jit(solution)/shard_map/all_to_all | solution.py:192
  786.0 3.9 reduce_sum.188
  789.9 0.7 copy.137
  790.7 1.9 dynamic-slice_bitcast_fusion
  (97 shorter events, 6.4 us)
Async XLA Ops:
  7.2 22.9 %copy-start = (bf16[1280,1280]{1,0:T(8,128)(2,1)S(1)}, bf16[1280,1280]{1,0:T(8,128)(2,1)}, u32[]{:S(2)}) copy-start(bf16[1280,1280]{1,0:T(8,128)(2,1)} %param.18) | copy-start | bytes 9830404
  7.2 113.7 %all-gather.9.cloned.1.call-start = ((), (), s32[]{:S(2)}) async-start(), calls=%async_computation.6 | async-start | bytes 10649600 | tf_op jit(solution)/shard_map/all_gather | solution.py:117
  9.6 11.7 %copy-start.13 = (s32[1,3]{1,0:T(1,128)S(1)}, s32[1,3]{1,0:T(1,128)}, u32[]{:S(2)}) copy-start(s32[1,3]{1,0:T(1,128)} %param.15) | copy-start | bytes 40
  16.2 13.9 %copy-start.3 = (bf16[64,1280]{1,0:T(8,128)(2,1)S(1)}, bf16[64,1280]{1,0:T(8,128)(2,1)}, u32[]{:S(2)}) copy-start(bf16[64,1280]{1,0:T(8,128)(2,1)} %param.14) | copy-start | bytes 491524
  23.1 0.8 copy-start.15
  23.1 8.9 %copy-start.10 = (f32[1280]{0:T(1024)S(1)}, f32[1280]{0:T(1024)}, u32[]{:S(2)}) copy-start(f32[1280]{0:T(1024)} %param.19) | copy-start | bytes 15364
  23.9 9.1 %copy-start.16 = (u32[128]{0:T(128)S(1)}, u32[128]{0:T(128)}, u32[]{:S(2)}) copy-start(u32[128]{0:T(128)} %constant.73) | copy-start | bytes 1540
  23.9 10.3 %copy-start.14 = (s32[16,1]{0,1:T(1,128)S(1)}, s32[16,1]{0,1:T(1,128)}, u32[]{:S(2)}) copy-start(s32[16,1]{0,1:T(1,128)} %param.21) | copy-start | bytes 196
  32.9 183.3 %reduce-scatter.5.cloned.1.call-start = ((), (), s32[]{:S(2)}) async-start(), calls=%async_computation.7 | async-start | bytes 8912896 | tf_op jit(solution)/shard_map/reduce_scatter | solution.py:136
  131.6 84.6 %copy-start.9 = (bf16[128,2048]{1,0:T(8,128)(2,1)S(1)}, bf16[128,2048]{1,0:T(8,128)(2,1)}, u32[]{:S(2)}) copy-start(bf16[128,2048]{1,0:T(8,128)(2,1)} %param.22) | copy-start | bytes 1572868
  131.7 101.1 %copy-start.11 = (s32[1,3]{1,0:T(1,128)S(1)}, s32[1,3]{1,0:T(1,128)}, u32[]{:S(2)}) copy-start(s32[1,3]{1,0:T(1,128)} %param.23) | copy-start | bytes 40
  131.7 267.0 %copy-start.12 = (f32[1,8192]{1,0:T(1,128)S(1)}, f32[1,8192]{1,0:T(1,128)}, u32[]{:S(2)}) copy-start(f32[1,8192]{1,0:T(1,128)} %param.24) | copy-start | bytes 98308
  131.7 98.0 %all-gather.11.cloned.1.call-start = ((), (), s32[]{:S(2)}) async-start(), calls=%async_computation.8 | async-start | bytes 1572864 | tf_op jit(solution)/shard_map/all_gather | solution.py:157
  218.2 46.0 %all-gather.13.cloned.1.call-start = ((), (), s32[]{:S(2)}) async-start(), calls=%async_computation.9 | async-start | bytes 2621440 | tf_op jit(solution)/shard_map/all_gather | solution.py:171
  231.6 167.1 %all-gather.15.cloned.1.call-start = ((), (), s32[]{:S(2)}) async-start(), calls=%async_computation.10 | async-start | bytes 22282240 | tf_op jit(solution)/shard_map/all_gather | solution.py:146
  232.2 279.5 %all-gather.17.cloned.1.call-start = ((), (), s32[]{:S(2)}) async-start(), calls=%async_computation.11 | async-start | bytes 17825792 | tf_op jit(solution)/shard_map/all_gather | solution.py:147
  232.7 321.6 %reduce-scatter.7.cloned.1.call-start = ((), (), s32[]{:S(2)}) async-start(), calls=%async_computation.12 | async-start | bytes 2621440 | tf_op jit(solution)/shard_map/reduce_scatter | solution.py:178
  511.7 42.6 %copy-start.4 = (bf16[256,2048]{1,0:T(8,128)(2,1)S(1)}, bf16[256,2048]{1,0:T(8,128)(2,1)}, u32[]{:S(2)}) copy-start(bf16[256,2048]{1,0:T(8,128)(2,1)} %all-gather.11.cloned.1.call-done) | copy-start | bytes 3145732
  524.5 66.0 %all-gather.19.cloned.1.call-start = ((), (), s32[]{:S(2)}) async-start(), calls=%async_computation.13 | async-start | bytes 2621440 | tf_op jit(solution)/shard_map/all_gather | solution.py:171
  555.5 3.3 collective-permute-start
  559.7 87.1 %reduce-scatter.9.cloned.1.call-start = ((), (), s32[]{:S(2)}) async-start(), calls=%async_computation.14 | async-start | bytes 2621440 | tf_op jit(solution)/shard_map/reduce_scatter | solution.py:178
  559.8 3.1 collective-permute-start.1
  604.0 42.7 %copy-start.2 = (bf16[128,2048]{1,0:T(8,128)(2,1)S(1)}, bf16[128,2048]{1,0:T(8,128)(2,1)}, u32[]{:S(2)}) copy-start(bf16[128,2048]{1,0:T(8,128)(2,1)} %slice_select_fusion.1) | copy-start | bytes 1572868
  616.8 35.3 %copy-start.8 = (bf16[128,2048]{1,0:T(8,128)(2,1)S(1)}, bf16[128,2048]{1,0:T(8,128)(2,1)}, u32[]{:S(2)}) copy-start(bf16[128,2048]{1,0:T(8,128)(2,1)} %param.27) | copy-start | bytes 1572868
  616.9 66.1 %all-gather.21.cloned.1.call-start = ((), (), s32[]{:S(2)}) async-start(), calls=%async_computation.15 | async-start | bytes 2621440 | tf_op jit(solution)/shard_map/all_gather | solution.py:171
  647.9 7.3 copy-start.5
  648.0 3.3 collective-permute-start.2
  651.3 0.8 copy-start.6
  655.2 70.8 %all-to-all-start = ((bf16[16,64,2048]{2,1,0:T(8,128)(2,1)}), bf16[16,64,2048]{2,1,0:T(8,128)(2,1)}, u32[]{:S(2)}, u32[]{:S(2)}) async-start(bf16[16,64,2048]{2,1,0:T(8,128)(2,1)} %bitcast.188), calls=%async_computation.4 | async-start | bytes 8388608 | tf_op jit(solution)/shard_map/all_to_all | solution.py:193
  662.1 77.1 %reduce-scatter.11.cloned.1.call-start = ((), (), s32[]{:S(2)}) async-start(), calls=%async_computation.16 | async-start | bytes 2621440 | tf_op jit(solution)/shard_map/reduce_scatter | solution.py:178
  662.1 2.8 collective-permute-start.3
  732.5 6.7 copy-start.7
  732.5 53.5 %all-to-all-start.1 = ((bf16[16,64,2048]{2,0,1:T(8,128)(2,1)}), bf16[16,64,2048]{2,0,1:T(8,128)(2,1)}, u32[]{:S(2)}, u32[]{:S(2)}) async-start(bf16[16,64,2048]{2,0,1:T(8,128)(2,1)} %copy.122), calls=%async_computation.5 | async-start | bytes 8388608 | tf_op jit(solution)/shard_map/all_to_all | solution.py:192
  737.5 53.2 %all-reduce.3.cloned.1.call-start = ((), (), s32[]{:S(2)}) async-start(), calls=%async_computation.17 | async-start | bytes 2097152 | tf_op jit(solution)/shard_map/psum | solution.py:25
  740.4 52.1 %copy-start.1 = (bf16[1280,1280]{1,0:T(8,128)(2,1)S(1)}, bf16[1280,1280]{1,0:T(8,128)(2,1)}, u32[]{:S(2)}) copy-start(bf16[1280,1280]{1,0:T(8,128)(2,1)} %param.18) | copy-start | bytes 9830404
Sparse Core Ops, SparseCore 0:
  33.0 87.8 all-gather.8
  131.8 84.4 reduce-scatter.4
  218.5 11.1 all-gather.10
  231.8 32.4 all-gather.12
  266.2 132.4 all-gather.14
  400.7 110.9 all-gather.16
  524.7 29.5 reduce-scatter.6
  559.8 30.6 all-gather.18
  617.0 29.7 reduce-scatter.8
  652.2 30.6 all-gather.20
  709.4 29.7 reduce-scatter.10
  742.9 26.6 all-reduce.2
where the time goes:
time: 808 us; the launch traced here: 800 us
  waiting for transfers between devices  590 us (73%)
  matrix products  97.5 us (12%)
  blocking collectives  27.2 us (3%)
  other arithmetic  27.1 us (3%)
  local copies, waits for them, and re-layouts  21.7 us (3%)
  starting transfers between devices  20.7 us (3%)
  between operations  15.5 us (2%)
    all_gather x1, waiting for transfers between devices, shards(): lax.all_gather(w_qkv, 'dp', axis=1, tiled=True)  132 us
    all_gather x1, waiting for transfers between devices, shards(): lax.all_gather(wo_t, 'dp', axis=1, tiled=True)  102 us
    reduce_scatter x1, waiting for transfers between devices, shards(): lax.psum_scatter(jnp.dot(picked, w_merge, preferred_element_type=jnp.floa...  83.8 us
    all_gather x3, waiting for transfers between devices, shards(): features = lax.all_gather(carried, 'mp', axis=1, tiled=True)  73.8 us
    reduce_scatter x3, waiting for transfers between devices, shards(): lax.psum_scatter(partial_value.astype(jnp.bfloat16), 'mp', scatter_dimens...  61.3 us
    all_gather x1, waiting for transfers between devices, shards(): lax.all_gather(merged, ('dp', 'mp'), axis=0, tiled=True)  60.5 us
    all_to_all x1, waiting for transfers between devices, shards(): lax.all_to_all(lax.all_to_all(outgoing, 'dp', split_axis=0, concat_axis=0...  43.2 us
    dot_general x3, matrix products, shards(): lax.dot_general(attended, out_weight, (((1,), (1,)), ((), ())), preferred...  38.4 us
  transfers between devices with their start and end apart: 18, of which 17 were waited for; matrix products, arithmetic and copies ran while one was open for 8% of the time, Pallas kernels for 0%

commit v1 on v0

--- a/solution.py
+++ b/solution.py
@@ -142,10 +142,16 @@
     present = jnp.sum((target == group_here).astype(jnp.int32))
     positions = jnp.arange(seq_rows, dtype=jnp.int32)
     entry_rows = jnp.where((positions < present)[:, None], image_rows, text)
-    gathered = (
-        lax.all_gather(w_qkv, "dp", axis=1, tiled=True),
-        lax.all_gather(wo_t, "dp", axis=1, tiled=True),
-    )
+    cells_pack = lambda piece_in, a_name, which_dim: jnp.concatenate(
+        jax.lax.all_to_all(
+            jnp.stack([piece_in] * jax.lax.axis_size(a_name)),
+            axis_name=a_name,
+            split_axis=0,
+            concat_axis=0,
+        ),
+        axis=which_dim,
+    )
+    gathered = (lax.all_gather(w_qkv, "dp", axis=1, tiled=True), cells_pack(wo_t, "dp", 1))
     qkv_weight = gathered[0][0]
     out_weight = gathered[1][0]
     norm_gain = lang_gain[0]

time: 808 us -> 907 us (1.12)
  waiting for transfers between devices: 590 us -> 676 us
    all_gather x1, waiting for transfers between devices: 132 us -> 318 us  [shards(): lax.all_gather(w_qkv, 'dp', axis=1, tiled=True)]
    all_gather x1 -> x0, waiting for transfers between devices: 102 us -> none  [shards(): lax.all_gather(wo_t, 'dp', axis=1, tiled=True)]
    reduce_scatter x3, waiting for transfers between devices: 61.3 us -> 76.3 us  [shards(): lax.psum_scatter(partial_value.astype(jnp.bfloat16), 'mp', scatter_dimens...]
    all_gather x3, waiting for transfers between devices: 73.8 us -> 61.3 us  [shards(): features = lax.all_gather(carried, 'mp', axis=1, tiled=True)]
  transfers between devices with their start and end apart: 18 -> 18, of which waited for: 17 -> 16; matrix products, arithmetic and copies ran while one was open for 8% -> 7% of each run, Pallas kernels for 0% -> 0%
where the time goes in v1:
time: 907 us; the launch traced here: 898 us
  waiting for transfers between devices  676 us (75%)
  matrix products  97.5 us (11%)
  local copies, waits for them, and re-layouts  27.7 us (3%)
  starting transfers between devices  27.7 us (3%)
  blocking collectives  27.2 us (3%)
  other arithmetic  27.1 us (3%)
  between operations  15.2 us (2%)
    all_gather x1, waiting for transfers between devices, shards(): lax.all_gather(w_qkv, 'dp', axis=1, tiled=True)  318 us
    reduce_scatter x1, waiting for transfers between devices, shards(): lax.psum_scatter(jnp.dot(picked, w_merge, preferred_element_type=jnp.floa...  83.8 us
    reduce_scatter x3, waiting for transfers between devices, shards(): lax.psum_scatter(partial_value.astype(jnp.bfloat16), 'mp', scatter_dimens...  76.3 us
    all_gather x3, waiting for transfers between devices, shards(): features = lax.all_gather(carried, 'mp', axis=1, tiled=True)  61.3 us
    all_gather x1, waiting for transfers between devices, shards(): lax.all_gather(merged, ('dp', 'mp'), axis=0, tiled=True)  60.5 us
    all_to_all x1, waiting for transfers between devices, shards(): lax.all_to_all(lax.all_to_all(outgoing, 'dp', split_axis=0, concat_axis=0...  43.2 us
    dot_general x3, matrix products, shards(): lax.dot_general(attended, out_weight, (((1,), (1,)), ((), ())), preferred...  38.4 us
    dot_general x3, matrix products, shards(): projected = jnp.dot(normed, qkv_weight, preferred_element_type=jnp.float32)  31.7 us
  transfers between devices with their start and end apart: 18, of which 16 were waited for; matrix products, arithmetic and copies ran while one was open for 7% of the time, Pallas kernels for 0%

profile of v1, /device:TPU:0, one launch (start us, length us, event | category | flops | bytes accessed | tf_op | source)
XLA Modules:
  0.0 898.1 jit_solution(7105874098749968875)
XLA Ops:
  7.2 1.2 convert_reduce_fusion.1
  8.4 1.1 fusion.61
  9.6 6.6 convolution_convert_fusion.4
  16.2 3.1 reshape.449
  19.3 2.0 fusion.82
  21.8 1.3 fusion.45
  23.3 0.6 copy-done.16
  23.9 2.4 fusion.49
  26.3 1.8 copy.109
  28.1 1.9 reshape.452
  30.0 1.7 fusion.84
  32.1 0.8 reshape.453
  33.0 0.6 dynamic-slice
  34.4 24.9 %all-reduce = s32[1024]{0:T(1024)S(1)} all-reduce(s32[1024]{0:T(1024)S(1)} %bitcast_dynamic-update-slice_fusion), channel_id=1, replica_groups=mesh['section'=2,'dp'=16,'mp'=4] {'dp','mp'}, use_global_device_ids=true, to_apply=%add | all-reduce | flops 1024 | bytes 8192 | tf_op jit(solution)/shard_map/squeeze | solution.py:120
  59.8 0.6 convert_reduce_fusion.2
  60.4 60.5 %all-gather.8.cloned.1.call-done = bf16[1024,5120]{1,0:T(8,128)(2,1)} async-done(((bf16[16,5120]{1,0:T(8,128)(2,1)}), bf16[1024,5120]{1,0:T(8,128)(2,1)}) %all-gather.8.cloned.1.call-update) | async-done | bytes 10485776 | tf_op jit(solution)/shard_map/all_gather | solution.py:117
  120.9 10.7 %convolution_convert_fusion.3 = bf16[2048,2048]{1,0:T(8,128)(2,1)} fusion(bf16[320,2048]{1,0:T(8,128)(2,1)} %param.20, s32[1024]{0:T(1024)S(1)} %get-tuple-element.7, bf16[1024,5120]{1,0:T(8,128)(2,1)} %all-gather.8.cloned.1.call-done, s32[]{:T(128)S(6)} %select_n.69), kind=kOutput, calls=%fused_computation.12 | convolution fusion | flops 4033478656 | bytes 10489860 | tf_op jit(solution)/shard_map/dot_general | solution.py:137
  131.7 0.8 iota_compare_fusion.13
  132.5 83.8 %reduce-scatter.5.cloned.1.call-done = bf16[128,2048]{1,0:T(8,128)(2,1)} async-done(((bf16[2048,2048]{1,0:T(8,128)(2,1)}), bf16[128,2048]{1,0:T(8,128)(2,1)}) %reduce-scatter.5.cloned.1.call-update) | async-done | bytes 524304 | tf_op jit(solution)/shard_map/reduce_scatter | solution.py:136
  216.2 2.0 broadcast_select_fusion
  218.3 11.4 %all-gather.10.cloned.1.call-done = bf16[256,2048]{1,0:T(8,128)(2,1)} async-done(((bf16[128,2048]{1,0:T(8,128)(2,1)}), bf16[256,2048]{1,0:T(8,128)(2,1)}) %all-gather.10.cloned.1.call-update) | async-done | bytes 1048592 | tf_op jit(solution)/shard_map/all_gather | solution.py:163
  229.7 1.9 slice_select_fusion
  232.2 6.0 stack.8
  238.2 7.1 all-to-all-start
  245.3 2.2 all-gather
  247.9 16.3 %all-gather.12.cloned.1.call-done = bf16[128,8192]{1,0:T(8,128)(2,1)} async-done(((bf16[128,2048]{1,0:T(8,128)(2,1)}), bf16[128,8192]{1,0:T(8,128)(2,1)}) %all-gather.12.cloned.1.call-update) | async-done | bytes 2097168 | tf_op jit(solution)/shard_map/all_gather | solution.py:177
  264.2 2.1 fusion.8
  266.3 317.7 %all-gather.14.cloned.1.call-done = bf16[1,8192,1280]{2,1,0:T(8,128)(2,1)} async-done(((bf16[1,512,1280]{2,1,0:T(8,128)(2,1)}), bf16[1,8192,1280]{2,1,0:T(8,128)(2,1)}) %all-gather.14.cloned.1.call-update) | async-done | bytes 20971536 | tf_op jit(solution)/shard_map/all_gather | solution.py:154
  584.0 10.6 %fusion.20 = bf16[128,1280]{1,0:T(8,128)(2,1)S(1)} fusion(bf16[1,8192,1280]{2,1,0:T(8,128)(2,1)} %all-gather.14.cloned.1.call-done, bf16[128,8192]{1,0:T(8,128)(2,1)} %all-gather.12.cloned.1.call-done, f32[8192]{0:T(1024)S(1)} %bitcast.196, f32[128]{0:T(128)S(1)} %add_rsqrt_fusion.2), kind=kOutput, calls=%fused_computation.35 | convolution fusion | flops 2688712704 | bytes 23429632 | tf_op jit(solution)/shard_map/dot_general | solution.py:179
  595.4 12.8 %convolution_convert_fusion.2 = bf16[128,8192]{1,0:T(8,128)(2,1)} fusion(bf16[128,1024]{0,1:T(8,128)(2,1)S(1)} %bitcast.190, bf16[8192,1024]{1,0:T(8,128)(2,1)} %bitcast.27), kind=kOutput, calls=%fused_computation.9 | convolution fusion | flops 2148532224 | bytes 19136512 | tf_op jit(solution)/shard_map/dot_general | solution.py:181
  608.3 44.8 %reduce-scatter.7.cloned.1.call-done = bf16[128,2048]{1,0:T(8,128)(2,1)} async-done(((bf16[128,8192]{1,0:T(8,128)(2,1)}), bf16[128,2048]{1,0:T(8,128)(2,1)}) %reduce-scatter.7.cloned.1.call-update) | async-done | bytes 524304 | tf_op jit(solution)/shard_map/reduce_scatter | solution.py:184
  653.1 1.2 add_convert_fusion.2
  654.3 1.8 collective-permute-start
  656.1 1.5 collective-permute-done
  657.6 0.8 slice_select_fusion.1
  658.5 2.5 collective-permute-start.1
  661.0 0.6 collective-permute-done.1
  662.0 27.3 %all-gather.16.cloned.1.call-done = bf16[128,8192]{1,0:T(8,128)(2,1)} async-done(((bf16[128,2048]{1,0:T(8,128)(2,1)}), bf16[128,8192]{1,0:T(8,128)(2,1)}) %all-gather.16.cloned.1.call-update) | async-done | bytes 2097168 | tf_op jit(solution)/shard_map/all_gather | solution.py:177
  689.3 2.1 fusion.11
  691.4 10.6 %fusion.23 = bf16[128,1280]{1,0:T(8,128)(2,1)S(1)} fusion(bf16[1,8192,1280]{2,1,0:T(8,128)(2,1)} %all-gather.14.cloned.1.call-done, bf16[128,8192]{1,0:T(8,128)(2,1)} %all-gather.16.cloned.1.call-done, f32[128]{0:T(128)S(1)} %add_rsqrt_fusion.1, f32[8192]{0:T(1024)S(1)} %bitcast.197), kind=kOutput, calls=%fused_computation.36 | convolution fusion | flops 2688712704 | bytes 23429632 | tf_op jit(solution)/shard_map/dot_general | solution.py:179
  702.8 12.8 %convolution_convert_fusion.1 = bf16[128,8192]{1,0:T(8,128)(2,1)} fusion(bf16[128,1024]{0,1:T(8,128)(2,1)S(1)} %bitcast.192, bf16[8192,1024]{1,0:T(8,128)(2,1)} %bitcast.27), kind=kOutput, calls=%fused_computation.8 | convolution fusion | flops 2148532224 | bytes 19136512 | tf_op jit(solution)/shard_map/dot_general | solution.py:181
  715.7 29.9 %reduce-scatter.9.cloned.1.call-done = bf16[128,2048]{1,0:T(8,128)(2,1)} async-done(((bf16[128,8192]{1,0:T(8,128)(2,1)}), bf16[128,2048]{1,0:T(8,128)(2,1)}) %reduce-scatter.9.cloned.1.call-update) | async-done | bytes 524304 | tf_op jit(solution)/shard_map/reduce_scatter | solution.py:184
  745.6 1.2 add_convert_fusion.1
  746.7 1.8 collective-permute-start.2
  748.6 1.5 collective-permute-done.2
  750.1 0.8 copy-done.6
  750.9 3.1 convolution_convert_fusion.5
  754.0 6.9 all-to-all-start.1
  760.9 2.2 collective-permute-start.3
  763.1 0.6 collective-permute-done.3
  764.1 17.6 %all-gather.18.cloned.1.call-done = bf16[128,8192]{1,0:T(8,128)(2,1)} async-done(((bf16[128,2048]{1,0:T(8,128)(2,1)}), bf16[128,8192]{1,0:T(8,128)(2,1)}) %all-gather.18.cloned.1.call-update) | async-done | bytes 2097168 | tf_op jit(solution)/shard_map/all_gather | solution.py:177
  781.7 2.1 fusion.14
  783.8 10.6 %fusion.26 = bf16[128,1280]{1,0:T(8,128)(2,1)S(1)} fusion(bf16[1,8192,1280]{2,1,0:T(8,128)(2,1)} %all-gather.14.cloned.1.call-done, bf16[128,8192]{1,0:T(8,128)(2,1)} %all-gather.18.cloned.1.call-done, f32[128]{0:T(128)S(1)} %add_rsqrt_fusion, f32[8192]{0:T(1024)S(1)} %bitcast.198), kind=kOutput, calls=%fused_computation.37 | convolution fusion | flops 2688712704 | bytes 23429632 | tf_op jit(solution)/shard_map/dot_general | solution.py:179
  795.2 12.8 %convolution_convert_fusion = bf16[128,8192]{1,0:T(8,128)(2,1)} fusion(bf16[128,1024]{0,1:T(8,128)(2,1)S(1)} %bitcast.191, bf16[8192,1024]{1,0:T(8,128)(2,1)} %bitcast.27), kind=kOutput, calls=%fused_computation.7 | convolution fusion | flops 2148532224 | bytes 19136512 | tf_op jit(solution)/shard_map/dot_general | solution.py:181
  808.1 16.7 %all-to-all-done.1 = bf16[16,64,2048]{2,1,0:T(8,128)(2,1)} async-done(((bf16[16,64,2048]{2,1,0:T(8,128)(2,1)}), bf16[16,64,2048]{2,1,0:T(8,128)(2,1)}, u32[]{:S(2)}, u32[]{:S(2)}) %all-to-all-start.1) | async-done | bytes 4194336 | tf_op jit(solution)/shard_map/all_to_all | solution.py:199
  824.8 6.5 copy.122
  831.3 5.0 all-to-all-start.2
  836.3 1.7 reduce-scatter.11.cloned.1.call-done
  838.0 1.2 fusion.53
  839.2 2.4 maximum_select_fusion
  841.6 43.2 %all-to-all-done.2 = bf16[16,64,2048]{2,0,1:T(8,128)(2,1)} async-done(((bf16[16,64,2048]{2,0,1:T(8,128)(2,1)}), bf16[16,64,2048]{2,0,1:T(8,128)(2,1)}, u32[]{:S(2)}, u32[]{:S(2)}) %all-to-all-start.2) | async-done | bytes 4194336 | tf_op jit(solution)/shard_map/all_to_all | solution.py:198
  884.8 3.9 reduce_sum.188
  888.7 0.7 copy.137
  889.5 1.9 dynamic-slice_bitcast_fusion
  (99 shorter events, 6.4 us)
Async XLA Ops:
  7.2 22.9 %copy-start = (bf16[1280,1280]{1,0:T(8,128)(2,1)S(1)}, bf16[1280,1280]{1,0:T(8,128)(2,1)}, u32[]{:S(2)}) copy-start(bf16[1280,1280]{1,0:T(8,128)(2,1)} %param.18) | copy-start | bytes 9830404
  7.2 113.7 %all-gather.8.cloned.1.call-start = ((), (), s32[]{:S(2)}) async-start(), calls=%async_computation.7 | async-start | bytes 10649600 | tf_op jit(solution)/shard_map/all_gather | solution.py:117
  9.6 11.7 %copy-start.14 = (s32[1,3]{1,0:T(1,128)S(1)}, s32[1,3]{1,0:T(1,128)}, u32[]{:S(2)}) copy-start(s32[1,3]{1,0:T(1,128)} %param.15) | copy-start | bytes 40
  16.2 13.9 %copy-start.3 = (bf16[64,1280]{1,0:T(8,128)(2,1)S(1)}, bf16[64,1280]{1,0:T(8,128)(2,1)}, u32[]{:S(2)}) copy-start(bf16[64,1280]{1,0:T(8,128)(2,1)} %param.14) | copy-start | bytes 491524
  23.1 0.8 copy-start.16
  23.1 8.9 copy-start.11
  23.9 9.1 %copy-start.17 = (u32[128]{0:T(128)S(1)}, u32[128]{0:T(128)}, u32[]{:S(2)}) copy-start(u32[128]{0:T(128)} %constant.73) | copy-start | bytes 1540
  23.9 10.3 %copy-start.15 = (s32[16,1]{0,1:T(1,128)S(1)}, s32[16,1]{0,1:T(1,128)}, u32[]{:S(2)}) copy-start(s32[16,1]{0,1:T(1,128)} %param.21) | copy-start | bytes 196
  32.9 183.3 %reduce-scatter.5.cloned.1.call-start = ((), (), s32[]{:S(2)}) async-start(), calls=%async_computation.8 | async-start | bytes 8912896 | tf_op jit(solution)/shard_map/reduce_scatter | solution.py:136
  131.6 84.6 %copy-start.10 = (bf16[128,2048]{1,0:T(8,128)(2,1)S(1)}, bf16[128,2048]{1,0:T(8,128)(2,1)}, u32[]{:S(2)}) copy-start(bf16[128,2048]{1,0:T(8,128)(2,1)} %param.22) | copy-start | bytes 1572868
  131.7 100.5 %copy-start.8 = (bf16[1,512,1024]{2,1,0:T(8,128)(2,1)S(1)}, bf16[1,512,1024]{2,1,0:T(8,128)(2,1)}, u32[]{:S(2)}) copy-start(bf16[1,512,1024]{2,1,0:T(8,128)(2,1)} %param.26) | copy-start | bytes 3145732
  131.7 98.0 %all-gather.10.cloned.1.call-start = ((), (), s32[]{:S(2)}) async-start(), calls=%async_computation.9 | async-start | bytes 1572864 | tf_op jit(solution)/shard_map/all_gather | solution.py:163
  218.2 46.0 %all-gather.12.cloned.1.call-start = ((), (), s32[]{:S(2)}) async-start(), calls=%async_computation.10 | async-start | bytes 2621440 | tf_op jit(solution)/shard_map/all_gather | solution.py:177
  231.6 352.4 %all-gather.14.cloned.1.call-start = ((), (), s32[]{:S(2)}) async-start(), calls=%async_computation.11 | async-start | bytes 22282240 | tf_op jit(solution)/shard_map/all_gather | solution.py:154
  238.2 7.2 copy-start.12
  238.2 345.8 %copy-start.13 = (f32[1,8192]{1,0:T(1,128)S(1)}, f32[1,8192]{1,0:T(1,128)}, u32[]{:S(2)}) copy-start(f32[1,8192]{1,0:T(1,128)} %param.24) | copy-start | bytes 98308
  238.2 357.2 %all-to-all-start = ((bf16[16,1,512,1024]{3,2,1,0:T(8,128)(2,1)}), bf16[16,1,512,1024]{3,2,1,0:T(8,128)(2,1)}, u32[]{:S(2)}, u32[]{:S(2)}) async-start(bf16[16,1,512,1024]{3,2,1,0:T(8,128)(2,1)} %stack.8), calls=%async_computation.1 | async-start | bytes 33554432 | tf_op jit(solution)/shard_map/all_to_all | solution.py:146
  245.3 407.8 %reduce-scatter.7.cloned.1.call-start = ((), (), s32[]{:S(2)}) async-start(), calls=%async_computation.12 | async-start | bytes 2621440 | tf_op jit(solution)/shard_map/reduce_scatter | solution.py:184
  595.4 57.7 %copy-start.4 = (bf16[256,2048]{1,0:T(8,128)(2,1)S(1)}, bf16[256,2048]{1,0:T(8,128)(2,1)}, u32[]{:S(2)}) copy-start(bf16[256,2048]{1,0:T(8,128)(2,1)} %all-gather.10.cloned.1.call-done) | copy-start | bytes 3145732
  608.3 81.0 %all-gather.16.cloned.1.call-start = ((), (), s32[]{:S(2)}) async-start(), calls=%async_computation.13 | async-start | bytes 2621440 | tf_op jit(solution)/shard_map/all_gather | solution.py:177
  654.3 3.3 collective-permute-start
  658.5 87.1 %reduce-scatter.9.cloned.1.call-start = ((), (), s32[]{:S(2)}) async-start(), calls=%async_computation.14 | async-start | bytes 2621440 | tf_op jit(solution)/shard_map/reduce_scatter | solution.py:184
  658.5 3.1 collective-permute-start.1
  702.8 42.7 %copy-start.2 = (bf16[128,2048]{1,0:T(8,128)(2,1)S(1)}, bf16[128,2048]{1,0:T(8,128)(2,1)}, u32[]{:S(2)}) copy-start(bf16[128,2048]{1,0:T(8,128)(2,1)} %slice_select_fusion.1) | copy-start | bytes 1572868
  715.6 35.3 %copy-start.9 = (bf16[128,2048]{1,0:T(8,128)(2,1)S(1)}, bf16[128,2048]{1,0:T(8,128)(2,1)}, u32[]{:S(2)}) copy-start(bf16[128,2048]{1,0:T(8,128)(2,1)} %param.27) | copy-start | bytes 1572868
  715.6 66.1 %all-gather.18.cloned.1.call-start = ((), (), s32[]{:S(2)}) async-start(), calls=%async_computation.15 | async-start | bytes 2621440 | tf_op jit(solution)/shard_map/all_gather | solution.py:177
  746.7 7.3 copy-start.5
  746.7 3.3 collective-permute-start.2
  750.1 0.8 copy-start.6
  754.0 70.8 %all-to-all-start.1 = ((bf16[16,64,2048]{2,1,0:T(8,128)(2,1)}), bf16[16,64,2048]{2,1,0:T(8,128)(2,1)}, u32[]{:S(2)}, u32[]{:S(2)}) async-start(bf16[16,64,2048]{2,1,0:T(8,128)(2,1)} %bitcast.180), calls=%async_computation.5 | async-start | bytes 8388608 | tf_op jit(solution)/shard_map/all_to_all | solution.py:199
  760.9 77.1 %reduce-scatter.11.cloned.1.call-start = ((), (), s32[]{:S(2)}) async-start(), calls=%async_computation.16 | async-start | bytes 2621440 | tf_op jit(solution)/shard_map/reduce_scatter | solution.py:184
  760.9 2.8 collective-permute-start.3
  831.3 6.7 copy-start.7
  831.3 53.5 %all-to-all-start.2 = ((bf16[16,64,2048]{2,0,1:T(8,128)(2,1)}), bf16[16,64,2048]{2,0,1:T(8,128)(2,1)}, u32[]{:S(2)}, u32[]{:S(2)}) async-start(bf16[16,64,2048]{2,0,1:T(8,128)(2,1)} %copy.122), calls=%async_computation.6 | async-start | bytes 8388608 | tf_op jit(solution)/shard_map/all_to_all | solution.py:198
  836.3 53.2 %all-reduce.3.cloned.1.call-start = ((), (), s32[]{:S(2)}) async-start(), calls=%async_computation.17 | async-start | bytes 2097152 | tf_op jit(solution)/shard_map/psum | solution.py:25
  839.2 52.2 %copy-start.1 = (bf16[1280,1280]{1,0:T(8,128)(2,1)S(1)}, bf16[1280,1280]{1,0:T(8,128)(2,1)}, u32[]{:S(2)}) copy-start(bf16[1280,1280]{1,0:T(8,128)(2,1)} %param.18) | copy-start | bytes 9830404
Sparse Core Ops, SparseCore 0:
  33.0 87.8 all-gather.7
  131.8 84.4 reduce-scatter.4
  218.5 11.1 all-gather.9
  231.8 32.4 all-gather.11
  266.2 317.7 all-gather.13
  608.4 44.6 reduce-scatter.6
  658.6 30.6 all-gather.15
  715.8 29.7 reduce-scatter.8
  751.0 30.6 all-gather.17
  808.2 29.7 reduce-scatter.10
  841.7 26.6 all-reduce.2
